TPU v7x, 32 devices: a whole 2x2x4 slice. The times are simulated.
32 devices in a mesh: prompt: 4 (over x, core), sample: 8 (over z, y).
Axes of the slice: x: 2, y: 2, z: 4, core: 2. Of those that a mesh axis runs over, the one named last changes fastest.
Arguments:
- latent: bfloat16 [1024, 576], P('prompt'), may hold values from -16 to 16
- queries: bfloat16 [1024, 128, 576], P('prompt', 'sample'), may hold values from -64 to 64
- cotangent: bfloat16 [1024, 128, 512], P('prompt', 'sample'), may hold values from -18 to 18
- suffix_out: bfloat16 [1024, 128, 512], P('prompt', 'sample'), may hold values from -6 to 6
- suffix_lse: bfloat16 [1024, 128], P('prompt', 'sample'), may hold values from 6 to 10
- rewards: float32 [4], replicated, may hold values from -5 to 5
- slot_sample: int32 [1024], P('prompt'), may hold values from 0 to 4, as said below
Outputs:
- query_grad: bfloat16 [1024, 128, 576], P('prompt', 'sample')
- latent_grad: float32 [1024, 576], P('prompt')
Inputs may be any that keep to these rules, and one draw needn't show every extreme that they name: `slot_sample`: on every device the live slots come first and the others hold 4. Read over the devices in order, the live slots' completion numbers never fall, and every completion has a slot. Exactly 512 slots are live in all, and some device has all 256 of its slots live.
All inputs are finite; a program needn't handle non-finite values.
Results may differ from a plain program's by a relative error of at most 0.006.
Values may be sent and summed in bfloat16 or wider, within the bound.
A program may use at most 128 MiB of HBM per device.

v0:
```python
import math

import jax
import jax.numpy as jnp
from jax import lax
from jax.sharding import PartitionSpec as P

ROPE = 64
NOPE = 128


def softmax_scale():
    return (0.1 * math.log(40.0) + 1.0) ** 2 / math.sqrt(NOPE + ROPE)


def attend(queries, scaled, suffix_out, suffix_lse, prefix_keys, factor):
    value_width = scaled.shape[-1]
    scores = factor * jnp.einsum(
        "thd,pd->thp", queries, prefix_keys, preferred_element_type=jnp.float32
    )
    row_max = jnp.max(scores, axis=2)
    prefix_lse = row_max + jnp.log(jnp.sum(jnp.exp(scores - row_max[..., None]), axis=2))
    tail_lse = suffix_lse.astype(jnp.float32)
    joint_max = jnp.maximum(prefix_lse, tail_lse)
    total_lse = joint_max + jnp.log(jnp.exp(prefix_lse - joint_max) + jnp.exp(tail_lse - joint_max))
    probability = jnp.exp(scores - total_lse[..., None])
    prob_grad = jnp.einsum(
        "thd,pd->thp", scaled, prefix_keys[:, :value_width], preferred_element_type=jnp.float32
    )
    suffix_dot = jnp.sum(scaled.astype(jnp.float32) * suffix_out.astype(jnp.float32), axis=2)
    row_delta = (
        jnp.sum(probability * prob_grad, axis=2) + jnp.exp(tail_lse - total_lse) * suffix_dot
    )
    score_grad = (factor * probability * (prob_grad - row_delta[..., None])).astype(jnp.bfloat16)
    weights = probability.astype(jnp.bfloat16)
    query_grad = jnp.einsum(
        "thp,pd->thd", score_grad, prefix_keys, preferred_element_type=jnp.float32
    ).astype(jnp.bfloat16)

    def term_rows(first_row, row_count):
        key_term = jnp.einsum(
            "thp,thd->pd", score_grad, queries, preferred_element_type=jnp.float32
        )
        value_term = jnp.einsum("thp,thd->pd", weights, scaled, preferred_element_type=jnp.float32)
        return key_term + jnp.pad(value_term, ((0, 0), (0, key_term.shape[1] - value_width)))

    return (query_grad, term_rows)


def on_device(latent, queries, cotangent, suffix_out, suffix_lse, rewards, slot_sample):
    factor = softmax_scale()
    prefix_keys = lax.all_gather(latent, "prompt", axis=0, tiled=True)
    centred = rewards - jnp.mean(rewards)
    advantage_table = jnp.concatenate([centred, jnp.zeros((1,), jnp.float32)])
    sample_ids = jnp.arange(advantage_table.shape[0], dtype=jnp.int32)
    weight = jnp.sum(
        jnp.where(slot_sample[:, None] == sample_ids[None, :], advantage_table[None, :], 0.0),
        axis=1,
    )
    scaled = (weight[:, None, None] * cotangent.astype(jnp.float32)).astype(jnp.bfloat16)
    query_grad, term_rows = attend(queries, scaled, suffix_out, suffix_lse, prefix_keys, factor)
    prefix_count = prefix_keys.shape[0]
    owner_sums = lax.psum_scatter(
        term_rows(0, prefix_count), "prompt", scatter_dimension=0, tiled=True
    )
    latent_grad = lax.psum(owner_sums, "sample")
    return (query_grad, latent_grad)


def solution(mesh):
    in_specs = (
        P("prompt", None),
        P("prompt", "sample", None),
        P("prompt", "sample", None),
        P("prompt", "sample", None),
        P("prompt", "sample"),
        P(),
        P("prompt"),
    )
    out_specs = (P("prompt", "sample", None), P("prompt", None))
    return jax.shard_map(
        on_device, mesh=mesh, in_specs=in_specs, out_specs=out_specs, check_vma=False
    )
```

profile of v0, /device:TPU:0, one launch (start us, length us, event | category | flops | bytes accessed | tf_op | source)
XLA Modules:
  0.0 206.3 jit_solution(13262518655812535774)
XLA Ops:
  7.2 0.0 all-gather.2.cloned.1.call-start
  7.2 0.7 all-gather.2.cloned.1.call-update
  7.9 0.0 reduce-scatter.2.cloned.1.call-start
  7.9 1.3 reduce_sum.46
  9.9 0.7 broadcast_subtract_fusion
  10.5 0.1 pad_maximum_fusion
  10.6 0.8 select_reduce_fusion
  11.4 6.0 %multiply_reduce_fusion.2 = (f32[256,16]{1,0:T(8,128)S(1)}, bf16[256,16,512]{2,1,0:T(8,128)(2,1)}) fusion(bf16[256,16,512]{2,1,0:T(8,128)(2,1)} %param.10, bf16[256,16,512]{2,1,0:T(8,128)(2,1)} %param.9, f32[256]{0:T(256)S(1)} %select_reduce_fusion), kind=kLoop, calls=%fused_computation.7 | loop fusion | flops 14675968 | bytes 12600320 | tf_op jit(solution)/shard_map/reduce_sum | solution.py:30
  17.3 0.1 copy.25
  17.4 7.6 %copy.26 = bf16[256,16,512]{0,2,1:T(8,128)(2,1)} copy(bf16[256,16,512]{2,1,0:T(8,128)(2,1)} %get-tuple-element.3) | data formatting | bytes 8388608 | tf_op jit(solution)/shard_map/convert_element_type | solution.py:60
  25.0 4.9 %all-gather.2.cloned.1.call-done = bf16[1024,576]{0,1:T(8,128)(2,1)} async-done(((bf16[256,576]{0,1:T(8,128)(2,1)}), bf16[1024,576]{0,1:T(8,128)(2,1)}) %all-gather.2.cloned.1.call-update) | async-done | bytes 1179664 | tf_op jit(solution)/shard_map/all_gather | solution.py:52
  29.8 9.1 %multiply_reduce_fusion.1 = (f32[256,16]{0,1:T(8,128)S(1)}, f32[256,16,1024]{2,0,1:T(8,128)S(1)}) fusion(bf16[256,16,576]{0,2,1:T(8,128)(2,1)} %param.8, bf16[1024,576]{0,1:T(8,128)(2,1)} %all-gather.2.cloned.1.call-done), kind=kOutput, calls=%fused_computation.4 | convolution fusion | flops 4840222720 | bytes 22691840 | tf_op jit(solution)/shard_map/thd,pd->thp/dot_general | solution.py:18
  39.0 0.0 copy-start
  39.0 0.0 copy-start.4
  39.0 0.0 copy-start.1
  39.0 3.7 %exponential_reduce_fusion = f32[256,16]{0,1:T(8,128)S(1)} fusion(f32[256,16,1024]{2,0,1:T(8,128)S(1)} %get-tuple-element.5, f32[256,16]{0,1:T(8,128)S(1)} %get-tuple-element.4), kind=kLoop, calls=%fused_computation.3 | loop fusion | flops 12578816 | bytes 16809984 | tf_op jit(solution)/shard_map/reduce_sum | solution.py:22
  42.7 0.0 copy-done.4
  42.8 3.3 %copy-done = f32[256,16,1024]{2,0,1:T(8,128)} copy-done((f32[256,16,1024]{2,0,1:T(8,128)}, f32[256,16,1024]{2,0,1:T(8,128)S(1)}, u32[]{:S(2)}) %copy-start) | copy-done | bytes 16777240
  46.1 0.0 copy-done.1
  46.1 0.0 copy-start.3
  46.1 6.2 %fusion.5 = f32[1024,512]{0,1:T(8,128)} fusion(bf16[256,16,512]{0,2,1:T(8,128)(2,1)S(1)} %copy-done.1, f32[256,16,1024]{2,0,1:T(8,128)S(1)} %get-tuple-element.5, f32[256,16]{0,1:T(8,128)S(1)} %fusion.12), kind=kOutput, calls=%fused_computation.13 | convolution fusion | flops 4307550208 | bytes 23085056 | tf_op jit(solution)/shard_map/thp,thd->pd/dot_general | solution.py:44
  52.3 0.0 copy-done.3
  52.3 0.0 slice-start
  52.3 13.5 %multiply_reduce_fusion = (f32[256,16]{0,1:T(8,128)S(1)}, f32[256,16,1024]{2,0,1:T(8,128)}) fusion(f32[256,16,1024]{2,0,1:T(8,128)} %copy-done, f32[256,16]{0,1:T(8,128)S(1)} %fusion.12, bf16[256,16,512]{0,2,1:T(8,128)(2,1)S(1)} %copy-done.1, bf16[1024,576]{0,1:T(8,128)(2,1)S(1)} %copy-done.3), kind=kOutput, calls=%fused_computation.1 | convolution fusion | flops 4311740416 | bytes 38830080 | tf_op jit(solution)/shard_map/thd,pd->thp/dot_general | solution.py:27
  65.8 0.0 slice-start.1
  65.8 0.0 copy-start.5
  65.8 12.7 %multiply_convert_fusion = bf16[256,16,1024]{2,0,1:T(8,128)(2,1)S(1)} fusion(f32[256,16,1024]{2,0,1:T(8,128)} %get-tuple-element.7, f32[256,16,1024]{2,0,1:T(8,128)} %copy-done, f32[256,16]{0,1:T(8,128)S(1)} %fusion.20, f32[256,16]{0,1:T(8,128)S(1)} %fusion.12), kind=kLoop, calls=%fused_computation | loop fusion | flops 25165824 | bytes 41975808 | tf_op jit(solution)/shard_map/convert_element_type | solution.py:34
  78.6 0.0 copy-start.2
  78.6 3.2 %copy-done.2 = bf16[256,16,1024]{2,0,1:T(8,128)(2,1)} copy-done((bf16[256,16,1024]{2,0,1:T(8,128)(2,1)}, bf16[256,16,1024]{2,0,1:T(8,128)(2,1)S(1)}, u32[]{:S(2)}) %copy-start.2) | copy-done | bytes 8388632
  81.8 0.0 slice-done
  81.8 0.0 slice-done.1
  81.8 0.0 copy-done.5
  81.8 6.5 %bitcast_add_fusion = f32[1024,576]{0,1:T(8,128)} fusion(f32[1024,512]{0,1:T(8,128)S(1)} %copy-done.5, bf16[256,16,576]{0,2,1:T(8,128)(2,1)S(1)} %bitcast.23, bf16[256,16,1024]{2,0,1:T(8,128)(2,1)S(1)} %multiply_convert_fusion), kind=kOutput, calls=%fused_computation.12 | convolution fusion | flops 4832428032 | bytes 17563648 | tf_op jit(solution)/shard_map/thp,thd->pd/dot_general | solution.py:41
  88.3 0.0 reduce-scatter.2.cloned.1.call-update
  88.3 0.0 all-reduce.3.cloned.1.call-start
  88.4 32.9 %reduce-scatter.2.cloned.1.call-done = f32[256,576]{0,1:T(8,128)} async-done(((f32[1024,576]{0,1:T(8,128)}), f32[256,576]{0,1:T(8,128)}) %reduce-scatter.2.cloned.1.call-update) | async-done | bytes 589840 | tf_op jit(solution)/shard_map/reduce_scatter | solution.py:63
  121.3 0.0 all-reduce.3.cloned.1.call-update
  121.3 10.1 %convolution_convert_fusion = bf16[256,16,576]{0,2,1:T(8,128)(2,1)} fusion(bf16[256,16,1024]{2,0,1:T(8,128)(2,1)} %copy-done.2, bf16[1024,576]{0,1:T(8,128)(2,1)S(1)} %copy-done.3), kind=kOutput, calls=%fused_computation.11 | convolution fusion | flops 4834197504 | bytes 14286848 | tf_op jit(solution)/shard_map/thp,pd->thd/dot_general | solution.py:36
  131.4 66.5 %all-reduce.3.cloned.1.call-done = f32[256,576]{0,1:T(8,128)} async-done(((f32[256,576]{0,1:T(8,128)}), f32[256,576]{0,1:T(8,128)}) %all-reduce.3.cloned.1.call-update) | async-done | bytes 589840 | tf_op jit(solution)/shard_map/psum | solution.py:66
  197.9 1.9 copy.30
  (3 shorter events, 0.0 us)
Async XLA Ops:
  7.2 22.7 %all-gather.2.cloned.1.call-start = ((), (), s32[]{:S(2)}) async-start(), calls=%async_computation.1 | async-start | bytes 1474560 | tf_op jit(solution)/shard_map/all_gather | solution.py:52
  7.9 113.4 %reduce-scatter.2.cloned.1.call-start = ((), (), s32[]{:S(2)}) async-start(), calls=%async_computation.2 | async-start | bytes 2949120 | tf_op jit(solution)/shard_map/reduce_scatter | solution.py:63
  39.0 7.1 %copy-start = (f32[256,16,1024]{2,0,1:T(8,128)}, f32[256,16,1024]{2,0,1:T(8,128)S(1)}, u32[]{:S(2)}) copy-start(f32[256,16,1024]{2,0,1:T(8,128)S(1)} %get-tuple-element.5) | copy-start | bytes 50331652
  39.0 3.7 %copy-start.4 = (bf16[256,16]{0,1:T(8,128)(2,1)S(1)}, bf16[256,16]{0,1:T(8,128)(2,1)}, u32[]{:S(2)}) copy-start(bf16[256,16]{0,1:T(8,128)(2,1)} %param.11) | copy-start | bytes 24580
  39.0 7.1 %copy-start.1 = (bf16[256,16,512]{0,2,1:T(8,128)(2,1)S(1)}, bf16[256,16,512]{0,2,1:T(8,128)(2,1)}, u32[]{:S(2)}) copy-start(bf16[256,16,512]{0,2,1:T(8,128)(2,1)} %copy.26) | copy-start | bytes 12582916
  46.1 6.2 %copy-start.3 = (bf16[1024,576]{0,1:T(8,128)(2,1)S(1)}, bf16[1024,576]{0,1:T(8,128)(2,1)}, u32[]{:S(2)}) copy-start(bf16[1024,576]{0,1:T(8,128)(2,1)} %all-gather.2.cloned.1.call-done) | copy-start | bytes 3538948
  52.3 29.5 %slice-start = ((s8[4718592]{0:T(1024)(128)(4,1)}), s8[524288]{0:T(1024)(128)(4,1)S(1)}, s32[]{:S(2)}) async-start(s8[4718592]{0:T(1024)(128)(4,1)} %bitcast.22), calls=%async_computation.4 | async-start | bytes 1048576
  65.8 16.0 %slice-start.1 = ((s8[4718592]{0:T(1024)(128)(4,1)}), s8[4194304]{0:T(1024)(128)(4,1)S(1)}, s32[]{:S(2)}) async-start(s8[4718592]{0:T(1024)(128)(4,1)} %bitcast.22), calls=%async_computation.5 | async-start | bytes 8388608
  65.8 16.0 %copy-start.5 = (f32[1024,512]{0,1:T(8,128)S(1)}, f32[1024,512]{0,1:T(8,128)}, u32[]{:S(2)}) copy-start(f32[1024,512]{0,1:T(8,128)} %fusion.5) | copy-start | bytes 6291460
  78.6 3.2 %copy-start.2 = (bf16[256,16,1024]{2,0,1:T(8,128)(2,1)}, bf16[256,16,1024]{2,0,1:T(8,128)(2,1)S(1)}, u32[]{:S(2)}) copy-start(bf16[256,16,1024]{2,0,1:T(8,128)(2,1)S(1)} %multiply_convert_fusion) | copy-start | bytes 25165828
  88.3 109.6 %all-reduce.3.cloned.1.call-start = ((), (), s32[]{:S(2)}) async-start(), calls=%async_computation.3 | async-start | bytes 1179648 | tf_op jit(solution)/shard_map/psum | solution.py:66
Sparse Core Ops, SparseCore 0:
  9.5 20.2 all-gather.1
  88.4 32.7 reduce-scatter.1
  124.6 73.2 all-reduce.2
where the time goes:
time: 207 us; the launch traced here: 206 us
  waiting for transfers between devices  105 us (51%)
  matrix products  45.4 us (22%)
  other arithmetic  25.2 us (12%)
  local copies, waits for them, and re-layouts  16.1 us (8%)
  between operations  14.5 us (7%)
    psum x1, waiting for transfers between devices, on_device(): latent_grad = lax.psum(owner_sums, 'sample')  66.5 us
    reduce_scatter x1, waiting for transfers between devices, on_device(): lax.psum_scatter(term_rows(0, prefix_count), 'prompt', scatter_dimension=...  32.9 us
    dot_general x1, matrix products, attend(): jnp.einsum('thd,pd->thp', scaled, prefix_keys[:, :value_width], preferred...  13.5 us
    convert_element_type x1, other arithmetic, attend(): (factor * probability * (prob_grad - row_delta[..., None])).astype(jnp.bf...  12.7 us
    dot_general x1, matrix products, attend(): jnp.einsum('thp,pd->thd', score_grad, prefix_keys, preferred_element_type...  10.1 us
    dot_general x1, matrix products, attend(): jnp.einsum('thd,pd->thp', queries, prefix_keys, preferred_element_type=jn...  9.15 us
    unnamed x17, local copies, waits for them, and re-layouts  8.49 us
    convert_element_type x1, local copies, waits for them, and re-layouts, on_device(): (weight[:, None, None] * cotangent.astype(jnp.float32)).astype(jnp.bfloat16)  7.59 us
  transfers between devices with their start and end apart: 3, of which 3 were waited for; matrix products, arithmetic and copies ran while one was open for 13% of the time, Pallas kernels for 0%

commit v1 on v0

v1 whole, which is shorter than its diff:
```python
import functools
import math

import jax
import jax.numpy as jnp
from jax import lax
from jax.experimental import pallas as pl
from jax.experimental.pallas import tpu as pltpu
from jax.sharding import PartitionSpec as P

ROPE = 64
NOPE = 128
LOG2E = math.log2(math.e)


def softmax_scale():
    return (0.1 * math.log(40.0) + 1.0) ** 2 / math.sqrt(NOPE + ROPE)


def nt_dot(a, b):
    return lax.dot_general(a, b, (((1,), (1,)), ((), ())), preferred_element_type=jnp.float32)


def nn_dot(a, b):
    return jnp.dot(a, b, preferred_element_type=jnp.float32)


def attend_kernel(factor, keys_ref, q_ref, scaled_ref, dot_ref, lse_ref, dq_ref, acc_ref, keys_t_ref):
    step = pl.program_id(0)
    value_width = scaled_ref.shape[2]

    @pl.when(step == 0)
    def _():
        acc_ref[...] = jnp.zeros_like(acc_ref)
        keys_t_ref[...] = keys_ref[...].T

    q = q_ref[0]
    scaled = scaled_ref[0]
    suffix_dot = dot_ref[0]
    tail = lse_ref[0] * LOG2E
    scores = nn_dot(keys_ref[...], q) * (factor * LOG2E)
    joint = jnp.maximum(jnp.max(scores, axis=0, keepdims=True), tail)
    e = jnp.exp2(scores - joint)
    tail_e = jnp.exp2(tail - joint)
    inv = 1.0 / (jnp.sum(e, axis=0, keepdims=True) + tail_e)
    prob_grad = nt_dot(keys_ref[:, :value_width], scaled)
    delta = (jnp.sum(e * prob_grad, axis=0, keepdims=True) + tail_e * suffix_dot) * inv
    p = e * inv
    ds = (factor * p * (prob_grad - delta)).astype(jnp.bfloat16)
    weights = p.astype(jnp.bfloat16)
    dq_ref[0] = nn_dot(keys_t_ref[...], ds).astype(jnp.bfloat16)
    acc_ref[...] += nt_dot(ds, q)
    acc_ref[:, :value_width] += nn_dot(weights, scaled)


def attend(keys, queries, scaled, suffix_dot, suffix_lse):
    heads, width, slots = queries.shape
    value_width = scaled.shape[2]
    positions = keys.shape[0]
    return pl.pallas_call(
        functools.partial(attend_kernel, softmax_scale()),
        grid=(heads,),
        out_shape=(
            jax.ShapeDtypeStruct((heads, width, slots), jnp.bfloat16),
            jax.ShapeDtypeStruct((positions, width), jnp.float32),
        ),
        in_specs=[
            pl.BlockSpec((positions, width), lambda i: (0, 0)),
            pl.BlockSpec((1, width, slots), lambda i: (i, 0, 0)),
            pl.BlockSpec((1, slots, value_width), lambda i: (i, 0, 0)),
            pl.BlockSpec((1, 1, slots), lambda i: (i, 0, 0)),
            pl.BlockSpec((1, 1, slots), lambda i: (i, 0, 0)),
        ],
        out_specs=(
            pl.BlockSpec((1, width, slots), lambda i: (i, 0, 0)),
            pl.BlockSpec((positions, width), lambda i: (0, 0)),
        ),
        scratch_shapes=[pltpu.VMEM((width, positions), jnp.bfloat16)],
        compiler_params=pltpu.CompilerParams(vmem_limit_bytes=56 * 1024 * 1024),
        name="attend",
    )(keys, queries, scaled, suffix_dot, suffix_lse)


def on_device(latent, queries, cotangent, suffix_out, suffix_lse, rewards, slot_sample):
    keys = lax.all_gather(latent, "prompt", axis=0, tiled=True)
    centred = rewards - jnp.mean(rewards)
    advantage_table = jnp.concatenate([centred, jnp.zeros((1,), jnp.float32)])
    sample_ids = jnp.arange(advantage_table.shape[0], dtype=jnp.int32)
    weight = jnp.sum(
        jnp.where(slot_sample[:, None] == sample_ids[None, :], advantage_table[None, :], 0.0),
        axis=1,
    )
    scaled = (weight[:, None, None] * cotangent.astype(jnp.float32)).astype(jnp.bfloat16)
    suffix_dot = jnp.sum(scaled.astype(jnp.float32) * suffix_out.astype(jnp.float32), axis=2)
    dq, terms = attend(
        keys,
        jnp.transpose(queries, (1, 2, 0)),
        jnp.transpose(scaled, (1, 0, 2)),
        jnp.transpose(suffix_dot)[:, None, :],
        jnp.transpose(suffix_lse.astype(jnp.float32))[:, None, :],
    )
    owner_sums = lax.psum_scatter(terms, "prompt", scatter_dimension=0, tiled=True)
    return (jnp.transpose(dq, (2, 0, 1)), lax.psum(owner_sums, "sample"))


def solution(mesh):
    in_specs = (
        P("prompt", None),
        P("prompt", "sample", None),
        P("prompt", "sample", None),
        P("prompt", "sample", None),
        P("prompt", "sample"),
        P(),
        P("prompt"),
    )
    out_specs = (P("prompt", "sample", None), P("prompt", None))
    return jax.shard_map(
        on_device, mesh=mesh, in_specs=in_specs, out_specs=out_specs, check_vma=False
    )
```

time: 207 us -> 197 us (0.952)
  Pallas kernels: 0 us -> 45.5 us
  matrix products: 45.4 us -> 0 us
  waiting for transfers between devices: 105 us -> 118 us
  local copies, waits for them, and re-layouts: 16.1 us -> 5.2 us
  other arithmetic: 25.2 us -> 14.3 us
    pallas_call x0 -> x1, Pallas kernels: none -> 45.5 us  [attend(): pl.pallas_call(functools.partial(attend_kernel, softmax_scale()), grid=(h...]
    dot_general x5 -> x0, matrix products: 45.4 us -> none  [the longest x1 13.5 us: attend(): jnp.einsum('thd,pd->thp', scaled, prefix_keys[:, :value_width], preferred...]
    convert_element_type x1 -> x0, other arithmetic: 12.7 us -> none  [attend(): (factor * probability * (prob_grad - row_delta[..., None])).astype(jnp.bf...]
    psum x1, waiting for transfers between devices: 66.5 us -> 77.2 us  [on_device(): return (jnp.transpose(dq, (2, 0, 1)), lax.psum(owner_sums, 'sample'))]
    convert_element_type x1 -> x0, local copies, waits for them, and re-layouts: 7.59 us -> none  [on_device(): (weight[:, None, None] * cotangent.astype(jnp.float32)).astype(jnp.bfloat16)]
    unnamed x17 -> x2, local copies, waits for them, and re-layouts: 8.49 us -> 3.98 us
    reduce_sum x2 -> x1, other arithmetic: 9.65 us -> 10.8 us  [on_device(): jnp.sum(scaled.astype(jnp.float32) * suffix_out.astype(jnp.float32), axis=2)]
  transfers between devices with their start and end apart: 3 -> 3, of which waited for: 3 -> 3; matrix products, arithmetic and copies ran while one was open for 13% -> 8% of each run, Pallas kernels for 0% -> 0%
where the time goes in v1:
time: 197 us
  waiting for transfers between devices  118 us (60%)
  Pallas kernels  45.5 us (23%)
  between operations  14.4 us (7%)
  other arithmetic  14.3 us (7%)
  local copies, waits for them, and re-layouts  5.2 us (3%)
    psum x1, waiting for transfers between devices, on_device(): return (jnp.transpose(dq, (2, 0, 1)), lax.psum(owner_sums, 'sample'))  77.2 us
    pallas_call x1, Pallas kernels, attend(): pl.pallas_call(functools.partial(attend_kernel, softmax_scale()), grid=(h...  45.5 us
    reduce_scatter x1, waiting for transfers between devices, on_device(): lax.psum_scatter(terms, 'prompt', scatter_dimension=0, tiled=True)  34.6 us
    reduce_sum x1, other arithmetic, on_device(): jnp.sum(scaled.astype(jnp.float32) * suffix_out.astype(jnp.float32), axis=2)  10.8 us
    all_gather x1, waiting for transfers between devices, on_device(): keys = lax.all_gather(latent, 'prompt', axis=0, tiled=True)  5.72 us
    unnamed x2, local copies, waits for them, and re-layouts  3.98 us
  transfers between devices with their start and end apart: 3, of which 3 were waited for; matrix products, arithmetic and copies ran while one was open for 8% of the time, Pallas kernels for 0%

profile of v1, /device:TPU:0, one launch (start us, length us, event | category | flops | bytes accessed | tf_op | source)
XLA Modules:
  0.0 197.0 jit_solution(10871014740767908187)
XLA Ops:
  7.2 0.0 all-gather.2.cloned.1.call-start
  7.2 1.9 copy.13
  9.1 0.0 all-gather.2.cloned.1.call-update
  9.1 0.0 reduce-scatter.2.cloned.1.call-start
  9.1 0.7 convert_bitcast_fusion
  9.8 0.6 reshape.7.lse_ref
  10.5 1.3 reduce_sum.27
  12.4 0.7 broadcast_subtract_fusion
  13.0 0.1 pad_maximum_fusion
  13.1 0.8 select_reduce_fusion
  13.9 10.8 %multiply_reduce_fusion = (f32[256,16]{0,1:T(8,128)S(1)}, bf16[16,256,512]{2,1,0:T(8,128)(2,1)}) fusion(bf16[256,16,512]{2,1,0:T(8,128)(2,1)} %param.10, bf16[256,16,512]{2,1,0:T(8,128)(2,1)} %param.9, f32[256]{0:T(256)S(1)} %select_reduce_fusion), kind=kLoop, calls=%fused_computation | loop fusion | flops 14675968 | bytes 12600320 | tf_op jit(solution)/shard_map/reduce_sum | solution.py:94
  24.7 0.6 broadcast_in_dim.26.dot_ref
  25.3 5.7 %all-gather.2.cloned.1.call-done.keys_ref = bf16[1024,576]{1,0:T(8,128)(2,1)} async-done(((bf16[256,576]{1,0:T(8,128)(2,1)}), bf16[1024,576]{1,0:T(8,128)(2,1)}) %all-gather.2.cloned.1.call-update) | async-done | bytes 1179664 | tf_op jit(solution)/shard_map/all_gather | solution.py:85
  31.0 45.5 %attend.1 = (bf16[16,576,256]{2,1,0:T(8,128)(2,1)}, f32[1024,576]{1,0:T(8,128)}) custom-call(bf16[1024,576]{1,0:T(8,128)(2,1)} %all-gather.2.cloned.1.call-done.keys_ref, bf16[16,576,256]{2,1,0:T(8,128)(2,1)} %bitcast.7, bf16[16,256,512]{2,1,0:T(8,128)(2,1)} %get-tuple-element.11.scaled_ref, f32[16,1,256]{2,1,0:T(1,128)} %broadcast_in_dim.26.dot_ref, ...), custom_call_target="tpu_custom_call" | custom-call | tf_op jit(solution)/shard_map/attend/pallas_call | solution.py:60
  76.5 0.0 reduce-scatter.2.cloned.1.call-update
  76.5 0.0 all-reduce.2.cloned.1.call-start
  76.6 34.6 %reduce-scatter.2.cloned.1.call-done = f32[256,576]{1,0:T(8,128)} async-done(((f32[1024,576]{1,0:T(8,128)}), f32[256,576]{1,0:T(8,128)}) %reduce-scatter.2.cloned.1.call-update) | async-done | bytes 589840 | tf_op jit(solution)/shard_map/reduce_scatter | solution.py:102
  111.2 0.0 all-reduce.2.cloned.1.call-update
  111.2 77.2 %all-reduce.2.cloned.1.call-done = f32[256,576]{1,0:T(8,128)} async-done(((f32[256,576]{1,0:T(8,128)}), f32[256,576]{1,0:T(8,128)}) %all-reduce.2.cloned.1.call-update) | async-done | bytes 589840 | tf_op jit(solution)/shard_map/psum | solution.py:103
  188.4 2.1 %copy.16 = f32[256,576]{0,1:T(8,128)} copy(f32[256,576]{1,0:T(8,128)} %all-reduce.2.cloned.1.call-done) | data formatting | bytes 1179648
Async XLA Ops:
  7.2 23.9 %all-gather.2.cloned.1.call-start = ((), (), s32[]{:S(2)}) async-start(), calls=%async_computation.1 | async-start | bytes 1638400 | tf_op jit(solution)/shard_map/all_gather | solution.py:85
  9.1 102.1 %reduce-scatter.2.cloned.1.call-start = ((), (), s32[]{:S(2)}) async-start(), calls=%async_computation.2 | async-start | bytes 3276800 | tf_op jit(solution)/shard_map/reduce_scatter | solution.py:102
  76.5 111.8 %all-reduce.2.cloned.1.call-start = ((), (), s32[]{:S(2)}) async-start(), calls=%async_computation.3 | async-start | bytes 1310720 | tf_op jit(solution)/shard_map/psum | solution.py:103
Sparse Core Ops, SparseCore 0:
  10.1 20.8 all-gather.1
  76.6 34.4 reduce-scatter.1
  114.6 73.6 all-reduce.1

commit v2 on v1

--- a/solution.py
+++ b/solution.py
@@ -25,7 +25,7 @@
     return jnp.dot(a, b, preferred_element_type=jnp.float32)
 
 
-def attend_kernel(factor, keys_ref, q_ref, scaled_ref, dot_ref, lse_ref, dq_ref, acc_ref, keys_t_ref):
+def attend_kernel(factor, keys_ref, q_ref, scaled_ref, dot_ref, lse_ref, dq_ref, terms_ref, acc_ref, keys_t_ref):
     step = pl.program_id(0)
     value_width = scaled_ref.shape[2]
 
@@ -52,8 +52,12 @@
     acc_ref[...] += nt_dot(ds, q)
     acc_ref[:, :value_width] += nn_dot(weights, scaled)
 
-
-def attend(keys, queries, scaled, suffix_dot, suffix_lse):
+    @pl.when(step == pl.num_programs(0) - 1)
+    def _():
+        terms_ref[...] = acc_ref[...].astype(terms_ref.dtype)
+
+
+def attend(keys, queries, scaled, suffix_dot, suffix_lse, terms_type):
     heads, width, slots = queries.shape
     value_width = scaled.shape[2]
     positions = keys.shape[0]
@@ -62,7 +66,7 @@
         grid=(heads,),
         out_shape=(
             jax.ShapeDtypeStruct((heads, width, slots), jnp.bfloat16),
-            jax.ShapeDtypeStruct((positions, width), jnp.float32),
+            jax.ShapeDtypeStruct((positions, width), terms_type),
         ),
         in_specs=[
             pl.BlockSpec((positions, width), lambda i: (0, 0)),
@@ -75,14 +79,192 @@
             pl.BlockSpec((1, width, slots), lambda i: (i, 0, 0)),
             pl.BlockSpec((positions, width), lambda i: (0, 0)),
         ),
-        scratch_shapes=[pltpu.VMEM((width, positions), jnp.bfloat16)],
+        scratch_shapes=[
+            pltpu.VMEM((positions, width), jnp.float32),
+            pltpu.VMEM((width, positions), jnp.bfloat16),
+        ],
         compiler_params=pltpu.CompilerParams(vmem_limit_bytes=56 * 1024 * 1024),
         name="attend",
     )(keys, queries, scaled, suffix_dot, suffix_lse)
 
 
-def on_device(latent, queries, cotangent, suffix_out, suffix_lse, rewards, slot_sample):
-    keys = lax.all_gather(latent, "prompt", axis=0, tiled=True)
+MESH = pl.DeviceIdType.MESH
+
+
+def remote(src, dst, send_sem, recv_sem, target):
+    return pltpu.make_async_remote_copy(
+        src_ref=src, dst_ref=dst, send_sem=send_sem, recv_sem=recv_sem,
+        device_id=target, device_id_type=MESH,
+    )
+
+
+def greet(targets):
+    barrier = pltpu.get_barrier_semaphore()
+    for target in targets:
+        pl.semaphore_signal(barrier, inc=1, device_id=target, device_id_type=MESH)
+    pl.semaphore_wait(barrier, len(targets))
+
+
+def prompt_peers(chips):
+    me = lax.axis_index("prompt")
+    sample = lax.axis_index("sample")
+    chip, core = me // 2, me % 2
+    sibling = (chip * 2 + 1 - core, sample)
+    others = [lax.rem(chip + k, chips) for k in range(1, chips)]
+    return me, sample, chip, core, sibling, others
+
+
+def gather_kernel(chips, block_ref, keys_ref, far_ref, send_sem, recv_sem, pass_send, pass_recv, own_sem):
+    me, sample, chip, core, sibling, others = prompt_peers(chips)
+    targets = [(other * 2 + core, sample) for other in others]
+    greet([sibling] + targets)
+    own = pltpu.make_async_copy(block_ref, keys_ref.at[me], own_sem)
+    own.start()
+    far = []
+    for k, target in enumerate(targets):
+        copy = remote(block_ref, far_ref.at[k], send_sem.at[k], recv_sem.at[k], target)
+        copy.start()
+        far.append(copy)
+    near = [remote(block_ref, keys_ref.at[me], pass_send.at[0], pass_recv.at[0], sibling)]
+    near[0].start()
+    kept = []
+    for k in range(chips - 1):
+        far[k].wait_recv()
+        origin = lax.rem(chip - (k + 1) + chips, chips) * 2 + core
+        onward = remote(
+            far_ref.at[k], keys_ref.at[origin], pass_send.at[k + 1], pass_recv.at[k + 1], sibling
+        )
+        onward.start()
+        near.append(onward)
+        keep = pltpu.make_async_copy(far_ref.at[k], keys_ref.at[origin], send_sem.at[chips - 1 + k])
+        keep.start()
+        kept.append(keep)
+    own.wait()
+    for copy in far:
+        copy.wait_send()
+    for copy in kept:
+        copy.wait()
+    for copy in near:
+        copy.wait()
+
+
+def gather_keys(latent, n_prompt):
+    rows, width = latent.shape
+    chips = n_prompt // 2
+    vmem = pl.BlockSpec(memory_space=pltpu.VMEM)
+    dma = pltpu.SemaphoreType.DMA
+    keys = pl.pallas_call(
+        functools.partial(gather_kernel, chips),
+        out_shape=jax.ShapeDtypeStruct((n_prompt, rows, width), latent.dtype),
+        in_specs=[vmem],
+        out_specs=vmem,
+        scratch_shapes=[
+            pltpu.VMEM((chips - 1, rows, width), latent.dtype),
+            dma((2 * chips - 2,)), dma((chips - 1,)), dma((chips,)), dma((chips,)), dma,
+        ],
+        compiler_params=pltpu.CompilerParams(collective_id=0, has_side_effects=True),
+        name="gather_keys",
+    )(latent)
+    return keys.reshape(n_prompt * rows, width)
+
+
+def reduce_kernel(
+    chips, samples, terms_ref, out_ref,
+    near_ref, stage_ref, far_ref, part_ref, piece_ref, final_ref, full_ref,
+    near_send, near_recv, far_send, far_recv, piece_send, piece_recv, full_send, full_recv,
+):
+    me, sample, chip, core, sibling, others = prompt_peers(chips)
+    targets = [(other * 2 + core, sample) for other in others]
+    peers = [(me, lax.rem(sample + k, samples)) for k in range(1, samples)]
+    greet([sibling] + targets + peers)
+    wide = jnp.float32
+    narrow = terms_ref.dtype
+    order = others + [chip]
+
+    near = []
+    for k, other in enumerate(order):
+        copy = remote(
+            terms_ref.at[other * 2 + 1 - core], near_ref.at[k],
+            near_send.at[k], near_recv.at[k], sibling,
+        )
+        copy.start()
+        near.append(copy)
+    far = []
+    for k, other in enumerate(others):
+        near[k].wait_recv()
+        stage_ref[k] = (terms_ref[other * 2 + core].astype(wide) + near_ref[k].astype(wide)).astype(narrow)
+        copy = remote(stage_ref.at[k], far_ref.at[k], far_send.at[k], far_recv.at[k], targets[k])
+        copy.start()
+        far.append(copy)
+    near[-1].wait_recv()
+    total = terms_ref[me].astype(wide) + near_ref[chips - 1].astype(wide)
+    for k in range(chips - 1):
+        far[k].wait_recv()
+        total = total + far_ref[k].astype(wide)
+    part_ref[...] = total.reshape(part_ref.shape).astype(narrow)
+
+    pieces = []
+    for k, peer in enumerate(peers):
+        copy = remote(
+            part_ref.at[peer[1]], piece_ref.at[k], piece_send.at[k], piece_recv.at[k], peer
+        )
+        copy.start()
+        pieces.append(copy)
+    mine = part_ref[sample].astype(wide)
+    for k in range(samples - 1):
+        pieces[k].wait_recv()
+        mine = mine + piece_ref[k].astype(wide)
+    final_ref[...] = mine.astype(narrow)
+
+    spread = []
+    for k, peer in enumerate(peers):
+        copy = remote(final_ref, full_ref.at[k], full_send.at[k], full_recv.at[k], peer)
+        copy.start()
+        spread.append(copy)
+    out_ref[sample] = final_ref[...].astype(wide)
+    for k in range(samples - 1):
+        spread[k].wait_recv()
+        out_ref[lax.rem(sample - (k + 1) + samples, samples)] = full_ref[k].astype(wide)
+    for copy in near + far + pieces + spread:
+        copy.wait_send()
+
+
+def reduce_terms(terms, n_prompt, n_sample):
+    positions, width = terms.shape
+    rows = positions // n_prompt
+    chips = n_prompt // 2
+    chunk = rows // n_sample
+    vmem = pl.BlockSpec(memory_space=pltpu.VMEM)
+    dma = pltpu.SemaphoreType.DMA
+    kind = terms.dtype
+    out = pl.pallas_call(
+        functools.partial(reduce_kernel, chips, n_sample),
+        out_shape=jax.ShapeDtypeStruct((n_sample, chunk, width), jnp.float32),
+        in_specs=[vmem],
+        out_specs=vmem,
+        scratch_shapes=[
+            pltpu.VMEM((chips, rows, width), kind),
+            pltpu.VMEM((chips - 1, rows, width), kind),
+            pltpu.VMEM((chips - 1, rows, width), kind),
+            pltpu.VMEM((n_sample, chunk, width), kind),
+            pltpu.VMEM((n_sample - 1, chunk, width), kind),
+            pltpu.VMEM((chunk, width), kind),
+            pltpu.VMEM((n_sample - 1, chunk, width), kind),
+            dma((chips,)), dma((chips,)), dma((chips - 1,)), dma((chips - 1,)),
+            dma((n_sample - 1,)), dma((n_sample - 1,)), dma((n_sample - 1,)), dma((n_sample - 1,)),
+        ],
+        compiler_params=pltpu.CompilerParams(collective_id=1, has_side_effects=True),
+        name="reduce_terms",
+    )(terms.reshape(n_prompt, rows, width))
+    return out.reshape(rows, width)
+
+
+def on_device(n_prompt, n_sample, latent, queries, cotangent, suffix_out, suffix_lse, rewards, slot_sample):
+    direct = n_prompt % 2 == 0 and n_prompt > 2 and latent.shape[0] % (16 * n_sample) == 0
+    if direct:
+        keys = gather_keys(latent, n_prompt)
+    else:
+        keys = lax.all_gather(latent, "prompt", axis=0, tiled=True)
     centred = rewards - jnp.mean(rewards)
     advantage_table = jnp.concatenate([centred, jnp.zeros((1,), jnp.float32)])
     sample_ids = jnp.arange(advantage_table.shape[0], dtype=jnp.int32)
@@ -98,9 +280,13 @@
         jnp.transpose(scaled, (1, 0, 2)),
         jnp.transpose(suffix_dot)[:, None, :],
         jnp.transpose(suffix_lse.astype(jnp.float32))[:, None, :],
-    )
+        jnp.bfloat16 if direct else jnp.float32,
+    )
+    query_grad = jnp.transpose(dq, (2, 0, 1))
+    if direct:
+        return (query_grad, reduce_terms(terms, n_prompt, n_sample))
     owner_sums = lax.psum_scatter(terms, "prompt", scatter_dimension=0, tiled=True)
-    return (jnp.transpose(dq, (2, 0, 1)), lax.psum(owner_sums, "sample"))
+    return (query_grad, lax.psum(owner_sums, "sample"))
 
 
 def solution(mesh):
@@ -115,5 +301,6 @@
     )
     out_specs = (P("prompt", "sample", None), P("prompt", None))
     return jax.shard_map(
-        on_device, mesh=mesh, in_specs=in_specs, out_specs=out_specs, check_vma=False
-    )
+        functools.partial(on_device, mesh.shape["prompt"], mesh.shape["sample"]),
+        mesh=mesh, in_specs=in_specs, out_specs=out_specs, check_vma=False,
+    )

time: 197 us -> 114 us (0.58)
  waiting for transfers between devices: 118 us -> 0 us
  Pallas kernels: 45.5 us -> 91.8 us
  between operations: 14.4 us -> 1.3 us
    psum x1 -> x0, waiting for transfers between devices: 77.2 us -> none  [on_device(): return (jnp.transpose(dq, (2, 0, 1)), lax.psum(owner_sums, 'sample'))]
    pallas_call x0 -> x2, Pallas kernels: none -> 46.6 us  [the longest x1 31.7 us: reduce_terms(): pl.pallas_call(functools.partial(reduce_kernel, chips, n_sample), out_sha...]
    reduce_scatter x1 -> x0, waiting for transfers between devices: 34.6 us -> none  [on_device(): lax.psum_scatter(terms, 'prompt', scatter_dimension=0, tiled=True)]
    all_gather x1 -> x0, waiting for transfers between devices: 5.72 us -> none  [on_device(): keys = lax.all_gather(latent, 'prompt', axis=0, tiled=True)]
  transfers between devices with their start and end apart: 3 -> 0, of which waited for: 3 -> 0; matrix products, arithmetic and copies ran while one was open for 8% -> 0% of each run, Pallas kernels for 0% -> 0%
where the time goes in v2:
time: 114 us; the launch traced here: 113 us
  Pallas kernels  91.8 us (81%)
  other arithmetic  14.3 us (13%)
  local copies, waits for them, and re-layouts  5.2 us (5%)
  between operations  1.3 us (1%)
    pallas_call x1, Pallas kernels, attend(): pl.pallas_call(functools.partial(attend_kernel, softmax_scale()), grid=(h...  45.2 us
    pallas_call x1, Pallas kernels, reduce_terms(): pl.pallas_call(functools.partial(reduce_kernel, chips, n_sample), out_sha...  31.7 us
    pallas_call x1, Pallas kernels, gather_keys(): pl.pallas_call(functools.partial(gather_kernel, chips), out_shape=jax.Sha...  14.9 us
    reduce_sum x1, other arithmetic, on_device(): jnp.sum(scaled.astype(jnp.float32) * suffix_out.astype(jnp.float32), axis=2)  10.8 us
    unnamed x2, local copies, waits for them, and re-layouts  3.98 us

profile of v2, /device:TPU:0, one launch (start us, length us, event | category | flops | bytes accessed | tf_op | source)
XLA Modules:
  0.0 112.6 jit_solution(10080965834243556343)
XLA Ops:
  0.6 1.3 %reduce_sum.27 = f32[]{:T(128)} reduce(f32[4]{0:T(128)} %param.12, f32[]{:T(128)} %constant.1.clone.1), dimensions={0}, to_apply=%region_0.0 | reduce | flops 3 | bytes 24 | tf_op jit(solution)/shard_map/reduce_sum | solution.py:268
  2.5 0.7 broadcast_subtract_fusion
  3.2 0.1 pad_maximum_fusion
  3.3 0.8 select_reduce_fusion
  4.0 0.7 convert_bitcast_fusion
  4.7 0.6 reshape.19.lse_ref
  5.4 1.9 %copy.13.block_ref = bf16[256,576]{1,0:T(8,128)(2,1)} copy(bf16[256,576]{0,1:T(8,128)(2,1)} %param.7) | data formatting | bytes 589824 | tf_op args[0]
  7.2 14.9 %gather_keys.1 = bf16[4,256,576]{2,1,0:T(8,128)(2,1)} custom-call(bf16[256,576]{1,0:T(8,128)(2,1)} %copy.13.block_ref), custom_call_target="tpu_custom_call" | custom-call | tf_op jit(solution)/shard_map/gather_keys/pallas_call | solution.py:156
  22.1 10.8 %multiply_reduce_fusion = (f32[256,16]{0,1:T(8,128)S(1)}, bf16[16,256,512]{2,1,0:T(8,128)(2,1)}) fusion(bf16[256,16,512]{2,1,0:T(8,128)(2,1)} %param.10, bf16[256,16,512]{2,1,0:T(8,128)(2,1)} %param.9, f32[256]{0:T(256)S(1)} %select_reduce_fusion), kind=kLoop, calls=%fused_computation | loop fusion | flops 14675968 | bytes 12600320 | tf_op jit(solution)/shard_map/reduce_sum | solution.py:276
  32.9 0.6 broadcast_in_dim.26.dot_ref
  33.5 45.2 %attend.1 = (bf16[16,576,256]{2,1,0:T(8,128)(2,1)}, bf16[1024,576]{1,0:T(8,128)(2,1)}) custom-call(bf16[1024,576]{1,0:T(8,128)(2,1)} %bitcast.10, bf16[16,576,256]{2,1,0:T(8,128)(2,1)} %bitcast.11, bf16[16,256,512]{2,1,0:T(8,128)(2,1)} %get-tuple-element.11.scaled_ref, f32[16,1,256]{2,1,0:T(1,128)} %broadcast_in_dim.26.dot_ref, f32[16,1,256]{2,1,0:T(1,128)} %reshape.19.lse_ref), custom_call_target="tpu_custom_call" | custom-call | tf_op jit(solution)/shard_map/attend/pallas_call | solution.py:64
  78.7 31.7 %reduce_terms.1 = f32[8,32,576]{2,1,0:T(8,128)} custom-call(bf16[4,256,576]{2,1,0:T(8,128)(2,1)} %bitcast.13), custom_call_target="tpu_custom_call" | custom-call | tf_op jit(solution)/shard_map/reduce_terms/pallas_call | solution.py:240
  110.5 2.1 %copy.16 = f32[256,576]{0,1:T(8,128)} copy(f32[256,576]{1,0:T(8,128)} %bitcast.12) | data formatting | bytes 1179648

commit v3 on v2

--- a/solution.py
+++ b/solution.py
@@ -25,67 +25,86 @@
     return jnp.dot(a, b, preferred_element_type=jnp.float32)
 
 
-def attend_kernel(factor, keys_ref, q_ref, scaled_ref, dot_ref, lse_ref, dq_ref, terms_ref, acc_ref, keys_t_ref):
+GROUP = 4
+
+
+def attend_kernel(factor, count, *refs):
+    blocks = refs[:count]
+    q_ref, scaled_ref, dot_ref, lse_ref, dq_ref, terms_ref, acc_ref, keys_ref, keys_t_ref = refs[count:]
     step = pl.program_id(0)
-    value_width = scaled_ref.shape[2]
+    group, slots, value_width = scaled_ref.shape
 
     @pl.when(step == 0)
     def _():
         acc_ref[...] = jnp.zeros_like(acc_ref)
+        for k, block in enumerate(blocks):
+            rows = block.shape[0]
+            keys_ref[pl.ds(k * rows, rows), :] = block[...]
         keys_t_ref[...] = keys_ref[...].T
 
-    q = q_ref[0]
-    scaled = scaled_ref[0]
-    suffix_dot = dot_ref[0]
-    tail = lse_ref[0] * LOG2E
-    scores = nn_dot(keys_ref[...], q) * (factor * LOG2E)
-    joint = jnp.maximum(jnp.max(scores, axis=0, keepdims=True), tail)
-    e = jnp.exp2(scores - joint)
-    tail_e = jnp.exp2(tail - joint)
-    inv = 1.0 / (jnp.sum(e, axis=0, keepdims=True) + tail_e)
-    prob_grad = nt_dot(keys_ref[:, :value_width], scaled)
-    delta = (jnp.sum(e * prob_grad, axis=0, keepdims=True) + tail_e * suffix_dot) * inv
-    p = e * inv
-    ds = (factor * p * (prob_grad - delta)).astype(jnp.bfloat16)
-    weights = p.astype(jnp.bfloat16)
-    dq_ref[0] = nn_dot(keys_t_ref[...], ds).astype(jnp.bfloat16)
-    acc_ref[...] += nt_dot(ds, q)
-    acc_ref[:, :value_width] += nn_dot(weights, scaled)
+    grads, weights, queries = [], [], []
+    for h in range(group):
+        q = q_ref[h]
+        scaled = scaled_ref[h]
+        suffix_dot = dot_ref[h]
+        tail = lse_ref[h] * LOG2E
+        scores = nn_dot(keys_ref[...], q) * (factor * LOG2E)
+        prob_grad = nt_dot(keys_ref[:, :value_width], scaled)
+        joint = jnp.maximum(jnp.max(scores, axis=0, keepdims=True), tail)
+        e = jnp.exp2(scores - joint)
+        tail_e = jnp.exp2(tail - joint)
+        inv = 1.0 / (jnp.sum(e, axis=0, keepdims=True) + tail_e)
+        delta = (jnp.sum(e * prob_grad, axis=0, keepdims=True) + tail_e * suffix_dot) * inv
+        p = e * inv
+        ds = (factor * p * (prob_grad - delta)).astype(jnp.bfloat16)
+        dq_ref[h] = nn_dot(keys_t_ref[...], ds).astype(jnp.bfloat16)
+        grads.append(ds)
+        weights.append(p.astype(jnp.bfloat16))
+        queries.append(q.T)
+    joined = jnp.concatenate(grads, axis=1)
+    q_rows = jnp.concatenate(queries, axis=0)
+    scaled_rows = scaled_ref[...].reshape(group * slots, value_width)
+    acc_ref[:, :value_width] += nn_dot(
+        jnp.concatenate([joined] + weights, axis=1),
+        jnp.concatenate([q_rows[:, :value_width], scaled_rows], axis=0),
+    )
+    acc_ref[:, value_width:] += nn_dot(joined, q_rows[:, value_width:])
 
     @pl.when(step == pl.num_programs(0) - 1)
     def _():
         terms_ref[...] = acc_ref[...].astype(terms_ref.dtype)
 
 
-def attend(keys, queries, scaled, suffix_dot, suffix_lse, terms_type):
+def attend(blocks, queries, scaled, suffix_dot, suffix_lse, terms_type):
     heads, width, slots = queries.shape
     value_width = scaled.shape[2]
-    positions = keys.shape[0]
+    positions = sum(block.shape[0] for block in blocks)
+    group = math.gcd(heads, GROUP)
     return pl.pallas_call(
-        functools.partial(attend_kernel, softmax_scale()),
-        grid=(heads,),
+        functools.partial(attend_kernel, softmax_scale(), len(blocks)),
+        grid=(heads // group,),
         out_shape=(
             jax.ShapeDtypeStruct((heads, width, slots), jnp.bfloat16),
             jax.ShapeDtypeStruct((positions, width), terms_type),
         ),
-        in_specs=[
-            pl.BlockSpec((positions, width), lambda i: (0, 0)),
-            pl.BlockSpec((1, width, slots), lambda i: (i, 0, 0)),
-            pl.BlockSpec((1, slots, value_width), lambda i: (i, 0, 0)),
-            pl.BlockSpec((1, 1, slots), lambda i: (i, 0, 0)),
-            pl.BlockSpec((1, 1, slots), lambda i: (i, 0, 0)),
+        in_specs=[pl.BlockSpec(block.shape, lambda i: (0, 0)) for block in blocks] + [
+            pl.BlockSpec((group, width, slots), lambda i: (i, 0, 0)),
+            pl.BlockSpec((group, slots, value_width), lambda i: (i, 0, 0)),
+            pl.BlockSpec((group, 1, slots), lambda i: (i, 0, 0)),
+            pl.BlockSpec((group, 1, slots), lambda i: (i, 0, 0)),
         ],
         out_specs=(
-            pl.BlockSpec((1, width, slots), lambda i: (i, 0, 0)),
+            pl.BlockSpec((group, width, slots), lambda i: (i, 0, 0)),
             pl.BlockSpec((positions, width), lambda i: (0, 0)),
         ),
         scratch_shapes=[
             pltpu.VMEM((positions, width), jnp.float32),
+            pltpu.VMEM((positions, width), jnp.bfloat16),
             pltpu.VMEM((width, positions), jnp.bfloat16),
         ],
         compiler_params=pltpu.CompilerParams(vmem_limit_bytes=56 * 1024 * 1024),
         name="attend",
-    )(keys, queries, scaled, suffix_dot, suffix_lse)
+    )(*blocks, queries, scaled, suffix_dot, suffix_lse)
 
 
 MESH = pl.DeviceIdType.MESH
@@ -114,58 +133,12 @@
     return me, sample, chip, core, sibling, others
 
 
-def gather_kernel(chips, block_ref, keys_ref, far_ref, send_sem, recv_sem, pass_send, pass_recv, own_sem):
-    me, sample, chip, core, sibling, others = prompt_peers(chips)
-    targets = [(other * 2 + core, sample) for other in others]
-    greet([sibling] + targets)
-    own = pltpu.make_async_copy(block_ref, keys_ref.at[me], own_sem)
-    own.start()
-    far = []
-    for k, target in enumerate(targets):
-        copy = remote(block_ref, far_ref.at[k], send_sem.at[k], recv_sem.at[k], target)
-        copy.start()
-        far.append(copy)
-    near = [remote(block_ref, keys_ref.at[me], pass_send.at[0], pass_recv.at[0], sibling)]
-    near[0].start()
-    kept = []
-    for k in range(chips - 1):
-        far[k].wait_recv()
-        origin = lax.rem(chip - (k + 1) + chips, chips) * 2 + core
-        onward = remote(
-            far_ref.at[k], keys_ref.at[origin], pass_send.at[k + 1], pass_recv.at[k + 1], sibling
-        )
-        onward.start()
-        near.append(onward)
-        keep = pltpu.make_async_copy(far_ref.at[k], keys_ref.at[origin], send_sem.at[chips - 1 + k])
-        keep.start()
-        kept.append(keep)
-    own.wait()
-    for copy in far:
-        copy.wait_send()
-    for copy in kept:
-        copy.wait()
-    for copy in near:
-        copy.wait()
-
-
-def gather_keys(latent, n_prompt):
-    rows, width = latent.shape
-    chips = n_prompt // 2
-    vmem = pl.BlockSpec(memory_space=pltpu.VMEM)
-    dma = pltpu.SemaphoreType.DMA
-    keys = pl.pallas_call(
-        functools.partial(gather_kernel, chips),
-        out_shape=jax.ShapeDtypeStruct((n_prompt, rows, width), latent.dtype),
-        in_specs=[vmem],
-        out_specs=vmem,
-        scratch_shapes=[
-            pltpu.VMEM((chips - 1, rows, width), latent.dtype),
-            dma((2 * chips - 2,)), dma((chips - 1,)), dma((chips,)), dma((chips,)), dma,
-        ],
-        compiler_params=pltpu.CompilerParams(collective_id=0, has_side_effects=True),
-        name="gather_keys",
-    )(latent)
-    return keys.reshape(n_prompt * rows, width)
+def shifted_keys(latent, n_prompt):
+    blocks = [latent]
+    for k in range(1, n_prompt):
+        shift = [(i, (i + k) % n_prompt) for i in range(n_prompt)]
+        blocks.append(lax.ppermute(latent, "prompt", shift))
+    return blocks
 
 
 def reduce_kernel(
@@ -181,10 +154,13 @@
     narrow = terms_ref.dtype
     order = others + [chip]
 
+    def place(owner):
+        return lax.rem(me - owner + 2 * chips, 2 * chips)
+
     near = []
     for k, other in enumerate(order):
         copy = remote(
-            terms_ref.at[other * 2 + 1 - core], near_ref.at[k],
+            terms_ref.at[place(other * 2 + 1 - core)], near_ref.at[k],
             near_send.at[k], near_recv.at[k], sibling,
         )
         copy.start()
@@ -192,12 +168,12 @@
     far = []
     for k, other in enumerate(others):
         near[k].wait_recv()
-        stage_ref[k] = (terms_ref[other * 2 + core].astype(wide) + near_ref[k].astype(wide)).astype(narrow)
+        stage_ref[k] = (terms_ref[place(other * 2 + core)].astype(wide) + near_ref[k].astype(wide)).astype(narrow)
         copy = remote(stage_ref.at[k], far_ref.at[k], far_send.at[k], far_recv.at[k], targets[k])
         copy.start()
         far.append(copy)
     near[-1].wait_recv()
-    total = terms_ref[me].astype(wide) + near_ref[chips - 1].astype(wide)
+    total = terms_ref[0].astype(wide) + near_ref[chips - 1].astype(wide)
     for k in range(chips - 1):
         far[k].wait_recv()
         total = total + far_ref[k].astype(wide)
@@ -253,7 +229,7 @@
             dma((chips,)), dma((chips,)), dma((chips - 1,)), dma((chips - 1,)),
             dma((n_sample - 1,)), dma((n_sample - 1,)), dma((n_sample - 1,)), dma((n_sample - 1,)),
         ],
-        compiler_params=pltpu.CompilerParams(collective_id=1, has_side_effects=True),
+        compiler_params=pltpu.CompilerParams(collective_id=0, has_side_effects=True),
         name="reduce_terms",
     )(terms.reshape(n_prompt, rows, width))
     return out.reshape(rows, width)
@@ -262,9 +238,9 @@
 def on_device(n_prompt, n_sample, latent, queries, cotangent, suffix_out, suffix_lse, rewards, slot_sample):
     direct = n_prompt % 2 == 0 and n_prompt > 2 and latent.shape[0] % (16 * n_sample) == 0
     if direct:
-        keys = gather_keys(latent, n_prompt)
+        blocks = shifted_keys(latent, n_prompt)
     else:
-        keys = lax.all_gather(latent, "prompt", axis=0, tiled=True)
+        blocks = [lax.all_gather(latent, "prompt", axis=0, tiled=True)]
     centred = rewards - jnp.mean(rewards)
     advantage_table = jnp.concatenate([centred, jnp.zeros((1,), jnp.float32)])
     sample_ids = jnp.arange(advantage_table.shape[0], dtype=jnp.int32)
@@ -275,7 +251,7 @@
     scaled = (weight[:, None, None] * cotangent.astype(jnp.float32)).astype(jnp.bfloat16)
     suffix_dot = jnp.sum(scaled.astype(jnp.float32) * suffix_out.astype(jnp.float32), axis=2)
     dq, terms = attend(
-        keys,
+        blocks,
         jnp.transpose(queries, (1, 2, 0)),
         jnp.transpose(scaled, (1, 0, 2)),
         jnp.transpose(suffix_dot)[:, None, :],

time: 114 us -> 95.8 us (0.84)
  Pallas kernels: 91.8 us -> 71 us
  starting transfers between devices: 0 us -> 3.25 us
    pallas_call x2 -> x1, Pallas kernels: 60.1 us -> 39.8 us  [attend(): pl.pallas_call(functools.partial(attend_kernel, softmax_scale(), len(bloc...]
    ppermute x0 -> x3, starting transfers between devices: none -> 3.25 us  [shifted_keys(): blocks.append(lax.ppermute(latent, 'prompt', shift))]
    unnamed x2 -> x12, local copies, waits for them, and re-layouts: 3.98 us -> 4.25 us
  transfers between devices with their start and end apart: 0 -> 3, of which waited for: 0 -> 0; matrix products, arithmetic and copies ran while one was open for 0% -> 16% of each run, Pallas kernels for 0% -> 0%
where the time goes in v3:
time: 95.8 us; the launch traced here: 94.7 us
  Pallas kernels  71 us (74%)
  other arithmetic  13.6 us (14%)
  local copies, waits for them, and re-layouts  5.47 us (6%)
  starting transfers between devices  3.25 us (3%)
  between operations  1.34 us (1%)
    pallas_call x1, Pallas kernels, attend(): pl.pallas_call(functools.partial(attend_kernel, softmax_scale(), len(bloc...  39.8 us
    pallas_call x1, Pallas kernels, reduce_terms(): pl.pallas_call(functools.partial(reduce_kernel, chips, n_sample), out_sha...  31.3 us
    reduce_sum x1, other arithmetic, on_device(): jnp.sum(scaled.astype(jnp.float32) * suffix_out.astype(jnp.float32), axis=2)  10.8 us
    unnamed x12, local copies, waits for them, and re-layouts  4.25 us
    ppermute x3, starting transfers between devices, shifted_keys(): blocks.append(lax.ppermute(latent, 'prompt', shift))  3.25 us
  transfers between devices with their start and end apart: 3, of which 0 were waited for; matrix products, arithmetic and copies ran while one was open for 16% of the time, Pallas kernels for 0%

profile of v3, /device:TPU:0, one launch (start us, length us, event | category | flops | bytes accessed | tf_op | source)
XLA Modules:
  0.0 94.7 jit_solution(8657042862650072357)
XLA Ops:
  0.6 1.2 %copy.21.refs_0_ = bf16[256,576]{1,0:T(8,128)(2,1)S(1)} copy(bf16[256,576]{0,1:T(8,128)(2,1)} %param.7) | data formatting | bytes 589824 | tf_op args[0]
  1.8 0.0 copy-start
  1.8 2.5 %collective-permute-start.2 = (bf16[256,576]{1,0:T(8,128)(2,1)S(1)}, bf16[256,576]{1,0:T(8,128)(2,1)S(1)}, u32[]{:S(2)}, u32[]{:S(2)}) collective-permute-start(bf16[256,576]{1,0:T(8,128)(2,1)S(1)} %copy.21.refs_0_), channel_id=1, source_target_pairs={{0,24},{8,0},{16,8},{24,16},{1,25},{9,1},{17,9},{25,17},{2,26},{10... | collective-permute-start | bytes 884744 | tf_op jit(solution)/shard_map/ppermute | solution.py:140
  4.3 0.6 collective-permute-start.1
  4.9 0.2 collective-permute-start
  5.1 1.3 %reduce_sum.27 = f32[]{:T(128)} reduce(f32[4]{0:T(128)} %param.12, f32[]{:T(128)} %constant.1.clone.1), dimensions={0}, to_apply=%region_0.0 | reduce | flops 3 | bytes 24 | tf_op jit(solution)/shard_map/reduce_sum | solution.py:244
  7.0 0.7 broadcast_subtract_fusion
  7.6 0.1 pad_maximum_fusion
  7.7 0.8 select_reduce_fusion
  8.5 0.0 copy-start.4
  8.5 10.8 %multiply_reduce_fusion = (f32[256,16]{0,1:T(8,128)S(1)}, bf16[16,256,512]{2,1,0:T(8,128)(2,1)}) fusion(bf16[256,16,512]{2,1,0:T(8,128)(2,1)} %param.10, bf16[256,16,512]{2,1,0:T(8,128)(2,1)} %param.9, f32[256]{0:T(256)S(1)} %select_reduce_fusion), kind=kLoop, calls=%fused_computation | loop fusion | flops 14675968 | bytes 12600320 | tf_op jit(solution)/shard_map/reduce_sum | solution.py:252
  19.3 0.0 copy-done
  19.3 0.0 copy-done.4
  19.3 0.6 reshape.15.refs_7_
  19.9 0.6 broadcast_in_dim.26.refs_6_
  20.5 0.0 collective-permute-done.2.refs_3_
  20.5 0.0 copy-start.1
  20.5 0.0 collective-permute-done.1.refs_2_
  20.5 0.0 copy-start.2
  20.5 0.0 collective-permute-done.refs_1_
  20.6 0.0 copy-start.3
  20.6 0.7 copy-done.1
  21.2 0.1 copy-done.2
  21.4 0.2 copy-done.3
  21.5 39.8 %attend.1 = (bf16[16,576,256]{2,1,0:T(8,128)(2,1)}, bf16[1024,576]{1,0:T(8,128)(2,1)}) custom-call(bf16[256,576]{1,0:T(8,128)(2,1)} %copy-done, bf16[256,576]{1,0:T(8,128)(2,1)} %copy-done.3, bf16[256,576]{1,0:T(8,128)(2,1)} %copy-done.2, bf16[256,576]{1,0:T(8,128)(2,1)} %copy-done.1, bf16[16,576,256]{2,1,0:T(8,128)(2,1)} %bitcast.9, ...), custom_call_target="tpu_custom_call" | custom-call | tf_op jit(solution)/shard_map/attend/pallas_call | solution.py:83
  61.3 31.3 %reduce_terms.1 = f32[8,32,576]{2,1,0:T(8,128)} custom-call(bf16[4,256,576]{2,1,0:T(8,128)(2,1)} %bitcast.11), custom_call_target="tpu_custom_call" | custom-call | tf_op jit(solution)/shard_map/reduce_terms/pallas_call | solution.py:216
  92.6 2.1 %copy.22 = f32[256,576]{0,1:T(8,128)} copy(f32[256,576]{1,0:T(8,128)} %bitcast.10) | data formatting | bytes 1179648
  (1 shorter events, 0.0 us)
Async XLA Ops:
  1.8 17.5 %copy-start = (bf16[256,576]{1,0:T(8,128)(2,1)}, bf16[256,576]{1,0:T(8,128)(2,1)S(1)}, u32[]{:S(2)}) copy-start(bf16[256,576]{1,0:T(8,128)(2,1)S(1)} %copy.21.refs_0_) | copy-start | bytes 884740
  1.8 18.7 %collective-permute-start.2 = (bf16[256,576]{1,0:T(8,128)(2,1)S(1)}, bf16[256,576]{1,0:T(8,128)(2,1)S(1)}, u32[]{:S(2)}, u32[]{:S(2)}) collective-permute-start(bf16[256,576]{1,0:T(8,128)(2,1)S(1)} %copy.21.refs_0_), channel_id=1, source_target_pairs={{0,24},{8,0},{16,8},{24,16},{1,25},{9,1},{17,9},{25,17},{2,26},{10... | collective-permute-start | bytes 884744 | tf_op jit(solution)/shard_map/ppermute | solution.py:140
  4.3 16.3 %collective-permute-start.1 = (bf16[256,576]{1,0:T(8,128)(2,1)S(1)}, bf16[256,576]{1,0:T(8,128)(2,1)S(1)}, u32[]{:S(2)}, u32[]{:S(2)}) collective-permute-start(bf16[256,576]{1,0:T(8,128)(2,1)S(1)} %copy.21.refs_0_), channel_id=1, source_target_pairs={{0,16},{8,24},{16,0},{24,8},{1,17},{9,25},{17,1},{25,9},{2,18},{10... | collective-permute-start | bytes 884744 | tf_op jit(solution)/shard_map/ppermute | solution.py:140
  4.9 15.6 %collective-permute-start = (bf16[256,576]{1,0:T(8,128)(2,1)S(1)}, bf16[256,576]{1,0:T(8,128)(2,1)S(1)}, u32[]{:S(2)}, u32[]{:S(2)}) collective-permute-start(bf16[256,576]{1,0:T(8,128)(2,1)S(1)} %copy.21.refs_0_), channel_id=1, source_target_pairs={{0,8},{8,16},{16,24},{24,0},{1,9},{9,17},{17,25},{25,1},{2,10},{10... | collective-permute-start | bytes 884744 | tf_op jit(solution)/shard_map/ppermute | solution.py:140
  8.5 10.8 %copy-start.4 = (bf16[256,16]{0,1:T(8,128)(2,1)S(1)}, bf16[256,16]{0,1:T(8,128)(2,1)}, u32[]{:S(2)}) copy-start(bf16[256,16]{0,1:T(8,128)(2,1)} %param.11) | copy-start | bytes 24580
  20.5 0.7 copy-start.1
  20.5 0.8 copy-start.2
  20.6 1.0 %copy-start.3 = (bf16[256,576]{1,0:T(8,128)(2,1)}, bf16[256,576]{1,0:T(8,128)(2,1)S(1)}, u32[]{:S(2)}) copy-start(bf16[256,576]{1,0:T(8,128)(2,1)S(1)} %collective-permute-done.refs_1_) | copy-start | bytes 884740

commit v4 on v3

--- a/solution.py
+++ b/solution.py
@@ -26,6 +26,7 @@
 
 
 GROUP = 4
+HALVES = 2
 
 
 def attend_kernel(factor, count, *refs):
@@ -158,49 +159,61 @@
         return lax.rem(me - owner + 2 * chips, 2 * chips)
 
     near = []
-    for k, other in enumerate(order):
-        copy = remote(
-            terms_ref.at[place(other * 2 + 1 - core)], near_ref.at[k],
-            near_send.at[k], near_recv.at[k], sibling,
-        )
-        copy.start()
-        near.append(copy)
+    for h in range(HALVES):
+        for k, other in enumerate(order):
+            i = h * chips + k
+            copy = remote(
+                terms_ref.at[place(other * 2 + 1 - core), h], near_ref.at[i],
+                near_send.at[i], near_recv.at[i], sibling,
+            )
+            copy.start()
+            near.append(copy)
     far = []
-    for k, other in enumerate(others):
-        near[k].wait_recv()
-        stage_ref[k] = (terms_ref[place(other * 2 + core)].astype(wide) + near_ref[k].astype(wide)).astype(narrow)
-        copy = remote(stage_ref.at[k], far_ref.at[k], far_send.at[k], far_recv.at[k], targets[k])
-        copy.start()
-        far.append(copy)
-    near[-1].wait_recv()
-    total = terms_ref[0].astype(wide) + near_ref[chips - 1].astype(wide)
-    for k in range(chips - 1):
-        far[k].wait_recv()
-        total = total + far_ref[k].astype(wide)
-    part_ref[...] = total.reshape(part_ref.shape).astype(narrow)
-
+    for h in range(HALVES):
+        for k, other in enumerate(others):
+            i = h * (chips - 1) + k
+            near[h * chips + k].wait_recv()
+            stage_ref[i] = (
+                terms_ref[place(other * 2 + core), h].astype(wide) + near_ref[h * chips + k].astype(wide)
+            ).astype(narrow)
+            copy = remote(stage_ref.at[i], far_ref.at[i], far_send.at[i], far_recv.at[i], targets[k])
+            copy.start()
+            far.append(copy)
     pieces = []
-    for k, peer in enumerate(peers):
-        copy = remote(
-            part_ref.at[peer[1]], piece_ref.at[k], piece_send.at[k], piece_recv.at[k], peer
-        )
-        copy.start()
-        pieces.append(copy)
-    mine = part_ref[sample].astype(wide)
-    for k in range(samples - 1):
-        pieces[k].wait_recv()
-        mine = mine + piece_ref[k].astype(wide)
-    final_ref[...] = mine.astype(narrow)
-
+    for h in range(HALVES):
+        near[h * chips + chips - 1].wait_recv()
+        total = terms_ref[0, h].astype(wide) + near_ref[h * chips + chips - 1].astype(wide)
+        for k in range(chips - 1):
+            i = h * (chips - 1) + k
+            far[i].wait_recv()
+            total = total + far_ref[i].astype(wide)
+        part_ref[h] = total.reshape(part_ref.shape[1:]).astype(narrow)
+        for k, peer in enumerate(peers):
+            i = h * (samples - 1) + k
+            copy = remote(
+                part_ref.at[h, peer[1]], piece_ref.at[i], piece_send.at[i], piece_recv.at[i], peer
+            )
+            copy.start()
+            pieces.append(copy)
     spread = []
-    for k, peer in enumerate(peers):
-        copy = remote(final_ref, full_ref.at[k], full_send.at[k], full_recv.at[k], peer)
-        copy.start()
-        spread.append(copy)
-    out_ref[sample] = final_ref[...].astype(wide)
-    for k in range(samples - 1):
-        spread[k].wait_recv()
-        out_ref[lax.rem(sample - (k + 1) + samples, samples)] = full_ref[k].astype(wide)
+    for h in range(HALVES):
+        mine = part_ref[h, sample].astype(wide)
+        for k in range(samples - 1):
+            i = h * (samples - 1) + k
+            pieces[i].wait_recv()
+            mine = mine + piece_ref[i].astype(wide)
+        final_ref[h] = mine.astype(narrow)
+        for k, peer in enumerate(peers):
+            i = h * (samples - 1) + k
+            copy = remote(final_ref.at[h], full_ref.at[i], full_send.at[i], full_recv.at[i], peer)
+            copy.start()
+            spread.append(copy)
+    for h in range(HALVES):
+        out_ref[h, sample] = final_ref[h].astype(wide)
+        for k in range(samples - 1):
+            i = h * (samples - 1) + k
+            spread[i].wait_recv()
+            out_ref[h, lax.rem(sample - (k + 1) + samples, samples)] = full_ref[i].astype(wide)
     for copy in near + far + pieces + spread:
         copy.wait_send()
 
@@ -209,34 +222,36 @@
     positions, width = terms.shape
     rows = positions // n_prompt
     chips = n_prompt // 2
-    chunk = rows // n_sample
+    half = rows // HALVES
+    chunk = half // n_sample
+    near, far, links = HALVES * chips, HALVES * (chips - 1), HALVES * (n_sample - 1)
     vmem = pl.BlockSpec(memory_space=pltpu.VMEM)
     dma = pltpu.SemaphoreType.DMA
     kind = terms.dtype
     out = pl.pallas_call(
         functools.partial(reduce_kernel, chips, n_sample),
-        out_shape=jax.ShapeDtypeStruct((n_sample, chunk, width), jnp.float32),
+        out_shape=jax.ShapeDtypeStruct((HALVES, n_sample, chunk, width), jnp.float32),
         in_specs=[vmem],
         out_specs=vmem,
         scratch_shapes=[
-            pltpu.VMEM((chips, rows, width), kind),
-            pltpu.VMEM((chips - 1, rows, width), kind),
-            pltpu.VMEM((chips - 1, rows, width), kind),
-            pltpu.VMEM((n_sample, chunk, width), kind),
-            pltpu.VMEM((n_sample - 1, chunk, width), kind),
-            pltpu.VMEM((chunk, width), kind),
-            pltpu.VMEM((n_sample - 1, chunk, width), kind),
-            dma((chips,)), dma((chips,)), dma((chips - 1,)), dma((chips - 1,)),
-            dma((n_sample - 1,)), dma((n_sample - 1,)), dma((n_sample - 1,)), dma((n_sample - 1,)),
+            pltpu.VMEM((near, half, width), kind),
+            pltpu.VMEM((far, half, width), kind),
+            pltpu.VMEM((far, half, width), kind),
+            pltpu.VMEM((HALVES, n_sample, chunk, width), kind),
+            pltpu.VMEM((links, chunk, width), kind),
+            pltpu.VMEM((HALVES, chunk, width), kind),
+            pltpu.VMEM((links, chunk, width), kind),
+            dma((near,)), dma((near,)), dma((far,)), dma((far,)),
+            dma((links,)), dma((links,)), dma((links,)), dma((links,)),
         ],
         compiler_params=pltpu.CompilerParams(collective_id=0, has_side_effects=True),
         name="reduce_terms",
-    )(terms.reshape(n_prompt, rows, width))
+    )(terms.reshape(n_prompt, HALVES, half, width))
     return out.reshape(rows, width)
 
 
 def on_device(n_prompt, n_sample, latent, queries, cotangent, suffix_out, suffix_lse, rewards, slot_sample):
-    direct = n_prompt % 2 == 0 and n_prompt > 2 and latent.shape[0] % (16 * n_sample) == 0
+    direct = n_prompt % 2 == 0 and n_prompt > 2 and latent.shape[0] % (16 * HALVES * n_sample) == 0
     if direct:
         blocks = shifted_keys(latent, n_prompt)
     else:

time: 95.8 us -> 93.2 us (0.973)
  Pallas kernels: 71 us -> 69.3 us
    pallas_call x1, Pallas kernels: 31.3 us -> 29.5 us  [reduce_terms(): pl.pallas_call(functools.partial(reduce_kernel, chips, n_sample), out_sha...]
where the time goes in v4:
time: 93.2 us; the launch traced here: 93 us
  Pallas kernels  69.3 us (74%)
  other arithmetic  13.6 us (15%)
  local copies, waits for them, and re-layouts  5.47 us (6%)
  starting transfers between devices  3.25 us (3%)
  between operations  1.34 us (1%)
    pallas_call x1, Pallas kernels, attend(): pl.pallas_call(functools.partial(attend_kernel, softmax_scale(), len(bloc...  39.8 us
    pallas_call x1, Pallas kernels, reduce_terms(): pl.pallas_call(functools.partial(reduce_kernel, chips, n_sample), out_sha...  29.5 us
    reduce_sum x1, other arithmetic, on_device(): jnp.sum(scaled.astype(jnp.float32) * suffix_out.astype(jnp.float32), axis=2)  10.8 us
    unnamed x12, local copies, waits for them, and re-layouts  4.25 us
    ppermute x3, starting transfers between devices, shifted_keys(): blocks.append(lax.ppermute(latent, 'prompt', shift))  3.25 us
  transfers between devices with their start and end apart: 3, of which 0 were waited for; matrix products, arithmetic and copies ran while one was open for 16% of the time, Pallas kernels for 0%

profile of v4, /device:TPU:0, one launch (start us, length us, event | category | flops | bytes accessed | tf_op | source)
XLA Modules:
  0.0 93.0 jit_solution(10127688431295056148)
XLA Ops:
  0.6 1.2 %copy.21.refs_0_ = bf16[256,576]{1,0:T(8,128)(2,1)S(1)} copy(bf16[256,576]{0,1:T(8,128)(2,1)} %param.7) | data formatting | bytes 589824 | tf_op args[0]
  1.8 0.0 copy-start
  1.8 2.5 %collective-permute-start.2 = (bf16[256,576]{1,0:T(8,128)(2,1)S(1)}, bf16[256,576]{1,0:T(8,128)(2,1)S(1)}, u32[]{:S(2)}, u32[]{:S(2)}) collective-permute-start(bf16[256,576]{1,0:T(8,128)(2,1)S(1)} %copy.21.refs_0_), channel_id=1, source_target_pairs={{0,24},{8,0},{16,8},{24,16},{1,25},{9,1},{17,9},{25,17},{2,26},{10... | collective-permute-start | bytes 884744 | tf_op jit(solution)/shard_map/ppermute | solution.py:141
  4.3 0.6 collective-permute-start.1
  4.9 0.2 collective-permute-start
  5.1 1.3 %reduce_sum.27 = f32[]{:T(128)} reduce(f32[4]{0:T(128)} %param.12, f32[]{:T(128)} %constant.1.clone.1), dimensions={0}, to_apply=%region_0.0 | reduce | flops 3 | bytes 24 | tf_op jit(solution)/shard_map/reduce_sum | solution.py:259
  7.0 0.7 broadcast_subtract_fusion
  7.6 0.1 pad_maximum_fusion
  7.7 0.8 select_reduce_fusion
  8.5 0.0 copy-start.4
  8.5 10.8 %multiply_reduce_fusion = (f32[256,16]{0,1:T(8,128)S(1)}, bf16[16,256,512]{2,1,0:T(8,128)(2,1)}) fusion(bf16[256,16,512]{2,1,0:T(8,128)(2,1)} %param.10, bf16[256,16,512]{2,1,0:T(8,128)(2,1)} %param.9, f32[256]{0:T(256)S(1)} %select_reduce_fusion), kind=kLoop, calls=%fused_computation | loop fusion | flops 14675968 | bytes 12600320 | tf_op jit(solution)/shard_map/reduce_sum | solution.py:267
  19.3 0.0 copy-done
  19.3 0.0 copy-done.4
  19.3 0.6 reshape.15.refs_7_
  19.9 0.6 broadcast_in_dim.26.refs_6_
  20.5 0.0 collective-permute-done.2.refs_3_
  20.5 0.0 copy-start.1
  20.5 0.0 collective-permute-done.1.refs_2_
  20.5 0.0 copy-start.2
  20.5 0.0 collective-permute-done.refs_1_
  20.6 0.0 copy-start.3
  20.6 0.7 copy-done.1
  21.2 0.1 copy-done.2
  21.4 0.2 copy-done.3
  21.5 39.8 %attend.1 = (bf16[16,576,256]{2,1,0:T(8,128)(2,1)}, bf16[1024,576]{1,0:T(8,128)(2,1)}) custom-call(bf16[256,576]{1,0:T(8,128)(2,1)} %copy-done, bf16[256,576]{1,0:T(8,128)(2,1)} %copy-done.3, bf16[256,576]{1,0:T(8,128)(2,1)} %copy-done.2, bf16[256,576]{1,0:T(8,128)(2,1)} %copy-done.1, bf16[16,576,256]{2,1,0:T(8,128)(2,1)} %bitcast.9, ...), custom_call_target="tpu_custom_call" | custom-call | tf_op jit(solution)/shard_map/attend/pallas_call | solution.py:84
  61.3 29.5 %reduce_terms.1 = f32[2,8,16,576]{3,2,1,0:T(8,128)} custom-call(bf16[4,2,128,576]{3,2,1,0:T(8,128)(2,1)} %bitcast.11), custom_call_target="tpu_custom_call" | custom-call | tf_op jit(solution)/shard_map/reduce_terms/pallas_call | solution.py:231
  90.8 2.1 %copy.22 = f32[256,576]{0,1:T(8,128)} copy(f32[256,576]{1,0:T(8,128)} %bitcast.10) | data formatting | bytes 1179648
  (1 shorter events, 0.0 us)
Async XLA Ops:
  1.8 17.5 %copy-start = (bf16[256,576]{1,0:T(8,128)(2,1)}, bf16[256,576]{1,0:T(8,128)(2,1)S(1)}, u32[]{:S(2)}) copy-start(bf16[256,576]{1,0:T(8,128)(2,1)S(1)} %copy.21.refs_0_) | copy-start | bytes 884740
  1.8 18.7 %collective-permute-start.2 = (bf16[256,576]{1,0:T(8,128)(2,1)S(1)}, bf16[256,576]{1,0:T(8,128)(2,1)S(1)}, u32[]{:S(2)}, u32[]{:S(2)}) collective-permute-start(bf16[256,576]{1,0:T(8,128)(2,1)S(1)} %copy.21.refs_0_), channel_id=1, source_target_pairs={{0,24},{8,0},{16,8},{24,16},{1,25},{9,1},{17,9},{25,17},{2,26},{10... | collective-permute-start | bytes 884744 | tf_op jit(solution)/shard_map/ppermute | solution.py:141
  4.3 16.3 %collective-permute-start.1 = (bf16[256,576]{1,0:T(8,128)(2,1)S(1)}, bf16[256,576]{1,0:T(8,128)(2,1)S(1)}, u32[]{:S(2)}, u32[]{:S(2)}) collective-permute-start(bf16[256,576]{1,0:T(8,128)(2,1)S(1)} %copy.21.refs_0_), channel_id=1, source_target_pairs={{0,16},{8,24},{16,0},{24,8},{1,17},{9,25},{17,1},{25,9},{2,18},{10... | collective-permute-start | bytes 884744 | tf_op jit(solution)/shard_map/ppermute | solution.py:141
  4.9 15.6 %collective-permute-start = (bf16[256,576]{1,0:T(8,128)(2,1)S(1)}, bf16[256,576]{1,0:T(8,128)(2,1)S(1)}, u32[]{:S(2)}, u32[]{:S(2)}) collective-permute-start(bf16[256,576]{1,0:T(8,128)(2,1)S(1)} %copy.21.refs_0_), channel_id=1, source_target_pairs={{0,8},{8,16},{16,24},{24,0},{1,9},{9,17},{17,25},{25,1},{2,10},{10... | collective-permute-start | bytes 884744 | tf_op jit(solution)/shard_map/ppermute | solution.py:141
  8.5 10.8 %copy-start.4 = (bf16[256,16]{0,1:T(8,128)(2,1)S(1)}, bf16[256,16]{0,1:T(8,128)(2,1)}, u32[]{:S(2)}) copy-start(bf16[256,16]{0,1:T(8,128)(2,1)} %param.11) | copy-start | bytes 24580
  20.5 0.7 copy-start.1
  20.5 0.8 copy-start.2
  20.6 1.0 %copy-start.3 = (bf16[256,576]{1,0:T(8,128)(2,1)}, bf16[256,576]{1,0:T(8,128)(2,1)S(1)}, u32[]{:S(2)}) copy-start(bf16[256,576]{1,0:T(8,128)(2,1)S(1)} %collective-permute-done.refs_1_) | copy-start | bytes 884740
